TPU v7x, 256 devices: a whole 4x4x8 slice. The times are simulated.
256 devices in a mesh: shift: 8 (over x, core), rows: 32 (over y, z).
Axes of the slice: x: 4, y: 4, z: 8, core: 2. Of those that a mesh axis runs over, the one named last changes fastest.
Arguments:
- neighbours: int32 [256, 8], P('rows'), may hold values from 0 to 255, as said below
- couplings: float32 [256, 8, 128, 128], P('rows'), may hold values from -0.01953125 to 0.01953125
- eigvectors: float32 [256, 128, 128], P('rows'), may hold values from -1 to 1, as said below
- eigvalues: float32 [256, 128], P('rows'), may hold values from -2.5 to 2.5
- start_block: float32 [32768, 128], P('rows'), may hold values from -240 to 240
Outputs:
- basis: float32 [32768, 128], P('rows')
- basis_image: float32 [32768, 128], P('rows')
- projected: float32 [128, 128], replicated
Inputs may be any that keep to these rules, and one draw needn't show every extreme that they name: Each block's 8 neighbours are distinct blocks other than itself, each within 8 blocks of it. `eigvectors`: each block's matrix has orthonormal columns up to rounding.
All inputs are finite; a program needn't handle non-finite values.
Results may differ from a plain program's by a relative error of at most 0.00025.
Values sent between devices are 32-bit elements; how exact they have to be, the bound alone decides.
A program may use at most 64 MiB of HBM per device.

v0:
```python
import jax
import jax.numpy as jnp
from jax import lax
from jax.sharding import PartitionSpec as P

SWEEPS = 3
radius = 1.0
damping = 0.8


def extended(block, sides, width):
    for axis, dim in sides:
        count = lax.axis_size(axis)
        forward = [(i, i + 1) for i in range(count - 1)]
        backward = [(target, source) for source, target in forward]
        low = lax.ppermute(
            lax.slice_in_dim(block, block.shape[dim] - width, None, axis=dim), axis, forward
        )
        high = lax.ppermute(lax.slice_in_dim(block, 0, width, axis=dim), axis, backward)
        block = jnp.concatenate([low, block, high], axis=dim)
    return block


def unrotate(vectors, field):
    return jnp.einsum("imn,imc->inc", vectors, field, precision=lax.Precision.HIGHEST)


def rotate(vectors, field):
    return jnp.einsum("inm,imc->inc", vectors, field, precision=lax.Precision.HIGHEST)


def shifted_inverse(vectors, values, field, real_part, imag_part):
    width = field.shape[-1] // 2
    spun = unrotate(vectors, field)
    offset = real_part - values
    denom = offset * offset + imag_part * imag_part
    scale_re = (offset / denom)[..., None]
    scale_im = (-imag_part / denom)[..., None]
    first = spun[..., :width]
    second = spun[..., width:]
    mixed = jnp.concatenate(
        [scale_re * first - scale_im * second, scale_re * second + scale_im * first], axis=-1
    )
    return rotate(vectors, mixed)


def diagonal_part(vectors, values, field):
    return rotate(vectors, values[..., None] * unrotate(vectors, field))


def coupled(near_blocks, couplings):
    return jnp.einsum("iknm,ikmc->inc", couplings, near_blocks, precision=lax.Precision.HIGHEST)


def product(left, right):
    return jnp.dot(left, right, precision=lax.Precision.HIGHEST)


def per_device(neighbours, couplings, eigvectors, eigvalues, start_block):
    blk_dev, blk = eigvalues.shape
    ncol = start_block.shape[1]
    rows_here = blk_dev * blk
    total = rows_here * lax.axis_size("rows")
    count = lax.axis_size("shift")
    angle = jnp.pi * (lax.axis_index("shift").astype(jnp.float32) + 0.5) / count
    real_part = radius * jnp.cos(angle)
    imag_part = radius * jnp.sin(angle)
    local_index = neighbours - (lax.axis_index("rows") * blk_dev - blk_dev)

    def operate_on(field, padded):
        blocks_all = padded.reshape(3 * blk_dev, blk, padded.shape[-1])
        near = blocks_all[local_index]
        return diagonal_part(eigvectors, eigvalues, field) + coupled(near, couplings)

    blocks_b = start_block.reshape(blk_dev, blk, ncol)
    rhs = jnp.concatenate([blocks_b, jnp.zeros_like(blocks_b)], axis=-1)
    iterate = damping * shifted_inverse(eigvectors, eigvalues, rhs, real_part, imag_part)
    for sweep in range(1, SWEEPS):
        first = iterate[..., :ncol]
        second = iterate[..., ncol:]
        shifted = jnp.concatenate(
            [real_part * first - imag_part * second, imag_part * first + real_part * second],
            axis=-1,
        )
        iterate_padded = extended(iterate.reshape(rows_here, 2 * ncol), (("rows", 0),), rows_here)
        resid = rhs - shifted + operate_on(iterate, iterate_padded)
        iterate = iterate + damping * shifted_inverse(
            eigvectors, eigvalues, resid, real_part, imag_part
        )
    contrib = real_part / count * iterate[..., :ncol] - imag_part / count * iterate[..., ncol:]
    contrib = contrib.reshape(rows_here, ncol)
    field = lax.psum(contrib, "shift")
    gram = lax.psum(product(field.T, field), "rows") / total
    factor = jnp.linalg.cholesky(gram)
    basis = jax.scipy.linalg.solve_triangular(factor, field.T, lower=True).T
    padded = extended(basis, (("rows", 0),), rows_here)
    image = operate_on(basis.reshape(blk_dev, blk, ncol), padded).reshape(rows_here, ncol)
    projected = lax.psum(product(basis.T, image), "rows") / total
    basis_image, projected = (image, projected)
    return (basis, basis_image, projected)


def solution(mesh):
    in_specs = (
        P("rows", None),
        P("rows", None, None, None),
        P("rows", None, None),
        P("rows", None),
        P("rows", None),
    )
    out_specs = (P("rows", None), P("rows", None), P())
    return jax.shard_map(
        per_device, mesh=mesh, in_specs=in_specs, out_specs=out_specs, check_vma=False
    )
```

profile of v0, /device:TPU:2, one launch (start us, length us, event | category | flops | bytes accessed | tf_op | source)
XLA Modules:
  0.0 556.1 jit_solution(6460307151305128019)
XLA Ops:
  12.9 4.8 collective-permute-start
  22.3 17.1 %collective-permute-done = f32[1024,256]{1,0:T(8,128)} collective-permute-done((f32[1024,256]{1,0:T(8,128)}, f32[1024,256]{1,0:T(8,128)}, u32[]{:S(2)}, u32[]{:S(2)}) %collective-permute-start) | collective-permute-done | bytes 1048608 | tf_op jit(solution)/shard_map/ppermute | solution.py:16
  39.4 5.1 collective-permute-done.1
  44.5 3.8 pad_maximum_fusion
  48.3 6.2 %gather_fusion = f32[64,128,256]{2,1,0:T(8,128)} fusion(f32[24,128,256]{2,1,0:T(8,128)} %bitcast.105, s32[1024]{0:T(1024)S(1)} %pad_clamp_fusion), kind=kCustom, calls=%fused_computation | custom fusion | bytes 16777472 | tf_op jit(solution)/shard_map/gather | solution.py:72
  54.5 17.7 %fusion.11 = f32[8,128,256]{1,2,0:T(8,128)S(1)} fusion(f32[8,256,128]{2,1,0:T(8,128)S(1)} %fusion.37, f32[8,8,128,256]{3,2,1,0:T(8,128)} %bitcast.108, f32[8,8,128,128]{3,2,1,0:T(8,128)} %param.6, f32[8,128,128]{1,2,0:T(8,128)S(1)} %copy.20, f32[8,128,128]{1,2,0:T(8,128)} %get-tuple-element.18, f32[8,128,128]{1,2,0:T(8,128)} %get-tuple-element.17), kind=kOutput, calls=%fused_computation.26 | convolution fusion | flops 3222274048 | bytes 16252928 | tf_op jit(solution)/shard_map/iknm,ikmc->inc/dot_general | solution.py:52
  75.8 4.0 collective-permute-start.2
  84.3 16.2 %collective-permute-done.2 = f32[1024,256]{1,0:T(8,128)} collective-permute-done((f32[1024,256]{1,0:T(8,128)}, f32[1024,256]{1,0:T(8,128)}, u32[]{:S(2)}, u32[]{:S(2)}) %collective-permute-start.2) | collective-permute-done | bytes 1048608 | tf_op jit(solution)/shard_map/ppermute | solution.py:16
  100.6 5.6 %collective-permute-done.3 = f32[1024,256]{1,0:T(8,128)} collective-permute-done((f32[1024,256]{1,0:T(8,128)}, f32[1024,256]{1,0:T(8,128)}, u32[]{:S(2)}, u32[]{:S(2)}) %collective-permute-start.3) | collective-permute-done | bytes 1048608 | tf_op jit(solution)/shard_map/ppermute | solution.py:19
  106.2 3.8 pad_maximum_fusion.1
  110.0 6.2 %gather_fusion.1 = f32[64,128,256]{2,1,0:T(8,128)} fusion(f32[24,128,256]{2,1,0:T(8,128)} %bitcast.106, s32[1024]{0:T(1024)S(1)} %pad_clamp_fusion), kind=kCustom, calls=%fused_computation.1 | custom fusion | bytes 16777472 | tf_op jit(solution)/shard_map/gather | solution.py:72
  116.2 17.3 %fusion.14 = f32[8,128,256]{1,2,0:T(8,128)S(1)} fusion(f32[8,256,128]{2,1,0:T(8,128)S(1)} %fusion.38, f32[8,8,128,256]{3,2,1,0:T(8,128)} %bitcast.107, f32[8,8,128,128]{3,2,1,0:T(8,128)} %param.6, f32[8,128,128]{1,2,0:T(8,128)S(1)} %copy.20, f32[8,128,128]{1,2,0:T(8,128)} %get-tuple-element.16, f32[8,128,128]{1,2,0:T(8,128)} %get-tuple-element.15), kind=kOutput, calls=%fused_computation.29 | convolution fusion | flops 3222274048 | bytes 16252928 | tf_op jit(solution)/shard_map/iknm,ikmc->inc/dot_general | solution.py:52
  137.0 65.0 %all-reduce.5.cloned.1.call-done = f32[1024,128]{1,0:T(8,128)} async-done(((f32[1024,128]{1,0:T(8,128)}), f32[1024,128]{1,0:T(8,128)}) %all-reduce.5.cloned.1.call-update) | async-done | bytes 524304 | tf_op jit(solution)/shard_map/psum | solution.py:92
  202.0 2.8 fusion.39
  205.1 143.7 %all-reduce.7.cloned.1.call-done = f32[128,128]{0,1:T(8,128)} async-done(((f32[128,128]{0,1:T(8,128)}), f32[128,128]{0,1:T(8,128)}) %all-reduce.7.cloned.1.call-update) | async-done | bytes 65552 | tf_op jit(solution)/shard_map/psum | solution.py:93
  350.5 11.7 %cholesky.16 = f32[128,128]{1,0:T(8,128)S(1)} custom-call(f32[128,128]{1,0:T(8,128)S(1)} %fusion.30), custom_call_target="Cholesky" | custom-call | tf_op jit(solution)/shard_map/jit(cholesky)/cholesky | solution.py:94
  363.6 9.8 %custom-call.7 = f32[1,128,128]{1,2,0:T(8,128)S(1)} custom-call(f32[1,128,128]{2,1,0:T(8,128)S(1)} %fusion.27), custom_call_target="InvertDiagBlocksLowerTriangular" | custom-call | tf_op jit(solution)/shard_map/jit(_solve_triangular)/triangular_solve | solution.py:95
  375.1 3.2 collective-permute-start.4
  380.5 4.7 collective-permute-done.4
  385.2 4.2 collective-permute-done.5
  390.6 1.9 copy.48
  392.5 2.8 gather_fusion.2
  395.3 8.1 %convolution_bitcast_fusion.4 = f32[8,128,128]{1,2,0:T(8,128)S(1)} fusion(f32[8,8,128,128]{3,2,1,0:T(8,128)} %bitcast.112, f32[8,8,128,128]{3,2,1,0:T(8,128)} %param.6), kind=kOutput, calls=%fused_computation.30 | convolution fusion | flops 1610612736 | bytes 8912896 | tf_op jit(solution)/shard_map/iknm,ikmc->inc/dot_general | solution.py:52
  407.2 140.5 %all-reduce.9.cloned.1.call-done = f32[128,128]{0,1:T(8,128)} async-done(((f32[128,128]{0,1:T(8,128)}), f32[128,128]{0,1:T(8,128)}) %all-reduce.9.cloned.1.call-update) | async-done | bytes 65552 | tf_op jit(solution)/shard_map/psum | solution.py:98
  (55 shorter events, 35.6 us)
Async XLA Ops:
  7.2 1.5 copy-start
  7.2 194.8 %all-reduce.5.cloned.1.call-start = ((), (), s32[]{:S(2)}) async-start(), calls=%async_computation | async-start | bytes 1048576 | tf_op jit(solution)/shard_map/psum | solution.py:92
  8.6 10.3 %copy-start.3 = (s32[8,8]{1,0:T(8,128)S(1)}, s32[8,8]{1,0:T(8,128)}, u32[]{:S(2)}) copy-start(s32[8,8]{1,0:T(8,128)} %param.5) | copy-start | bytes 772
  10.3 9.9 %copy-start.2 = (f32[8,128]{1,0:T(8,128)S(1)}, f32[8,128]{1,0:T(8,128)}, u32[]{:S(2)}) copy-start(f32[8,128]{1,0:T(8,128)} %param.8) | copy-start | bytes 12292
  12.9 26.5 %collective-permute-start = (f32[1024,256]{1,0:T(8,128)}, f32[1024,256]{1,0:T(8,128)}, u32[]{:S(2)}, u32[]{:S(2)}) collective-permute-start(f32[1024,256]{1,0:T(8,128)} %bitcast.3), channel_id=1, source_target_pairs={{0,1},{1,2},{2,3},{3,4},{4,5},{5,6},{6,7},{7,8},{8,9},{9,10},{10,1... | collective-permute-start | bytes 3145736 | tf_op jit(solution)/shard_map/ppermute | solution.py:16
  17.7 26.8 %collective-permute-start.1 = (f32[1024,256]{1,0:T(8,128)}, f32[1024,256]{1,0:T(8,128)}, u32[]{:S(2)}, u32[]{:S(2)}) collective-permute-start(f32[1024,256]{1,0:T(8,128)} %bitcast.3), channel_id=1, source_target_pairs={{1,0},{2,1},{3,2},{4,3},{5,4},{6,5},{7,6},{8,7},{9,8},{10,9},{11,1... | collective-permute-start | bytes 3145736 | tf_op jit(solution)/shard_map/ppermute | solution.py:19
  75.8 24.8 %collective-permute-start.2 = (f32[1024,256]{1,0:T(8,128)}, f32[1024,256]{1,0:T(8,128)}, u32[]{:S(2)}, u32[]{:S(2)}) collective-permute-start(f32[1024,256]{1,0:T(8,128)} %bitcast.11), channel_id=1, source_target_pairs={{0,1},{1,2},{2,3},{3,4},{4,5},{5,6},{6,7},{7,8},{8,9},{9,10},{10,1... | collective-permute-start | bytes 3145736 | tf_op jit(solution)/shard_map/ppermute | solution.py:16
  79.8 26.4 %collective-permute-start.3 = (f32[1024,256]{1,0:T(8,128)}, f32[1024,256]{1,0:T(8,128)}, u32[]{:S(2)}, u32[]{:S(2)}) collective-permute-start(f32[1024,256]{1,0:T(8,128)} %bitcast.11), channel_id=1, source_target_pairs={{1,0},{2,1},{3,2},{4,3},{5,4},{6,5},{7,6},{8,7},{9,8},{10,9},{11,1... | collective-permute-start | bytes 3145736 | tf_op jit(solution)/shard_map/ppermute | solution.py:19
  136.9 211.8 %all-reduce.7.cloned.1.call-start = ((), (), s32[]{:S(2)}) async-start(), calls=%async_computation.1 | async-start | bytes 131072 | tf_op jit(solution)/shard_map/psum | solution.py:93
  204.8 342.9 %all-reduce.9.cloned.1.call-start = ((), (), s32[]{:S(2)}) async-start(), calls=%async_computation.2 | async-start | bytes 131072 | tf_op jit(solution)/shard_map/psum | solution.py:98
  375.1 10.1 %collective-permute-start.4 = (f32[1024,128]{0,1:T(8,128)S(1)}, f32[1024,128]{0,1:T(8,128)S(1)}, u32[]{:S(2)}, u32[]{:S(2)}) collective-permute-start(f32[1024,128]{0,1:T(8,128)S(1)} %bitcast.113), channel_id=1, source_target_pairs={{0,1},{1,2},{2,3},{3,4},{4,5},{5,6},{6,7},{7,8},{8,9},{9,10},{10,1... | collective-permute-start | bytes 1572872 | tf_op jit(solution)/shard_map/ppermute | solution.py:16
  378.3 11.1 %collective-permute-start.5 = (f32[1024,128]{0,1:T(8,128)S(1)}, f32[1024,128]{0,1:T(8,128)S(1)}, u32[]{:S(2)}, u32[]{:S(2)}) collective-permute-start(f32[1024,128]{0,1:T(8,128)S(1)} %bitcast.114), channel_id=1, source_target_pairs={{1,0},{2,1},{3,2},{4,3},{5,4},{6,5},{7,6},{8,7},{9,8},{10,9},{11,1... | collective-permute-start | bytes 1572872 | tf_op jit(solution)/shard_map/ppermute | solution.py:19
  404.6 144.7 %copy-start.1 = (f32[8,128,128]{1,2,0:T(8,128)}, f32[8,128,128]{1,2,0:T(8,128)S(1)}, u32[]{:S(2)}) copy-start(f32[8,128,128]{1,2,0:T(8,128)S(1)} %convolution_add_fusion) | copy-start | bytes 1572868
Sparse Core Ops, SparseCore 0:
  137.1 64.8 all-reduce.4
  206.0 142.7 all-reduce.6
  406.4 141.3 all-reduce.8
where the time goes:
time: 562 us; the launch traced here: 556 us
  waiting for transfers between devices  402 us (72%)
  matrix products  61.7 us (11%)
  other arithmetic  37.6 us (7%)
  local copies, waits for them, and re-layouts  23.8 us (4%)
  starting transfers between devices  16.5 us (3%)
  between operations  14.5 us (3%)
    psum x1, waiting for transfers between devices, per_device(): gram = lax.psum(product(field.T, field), 'rows') / total  144 us
    psum x1, waiting for transfers between devices, per_device(): projected = lax.psum(product(basis.T, image), 'rows') / total  140 us
    psum x1, waiting for transfers between devices, per_device(): field = lax.psum(contrib, 'shift')  65 us
    dot_general x3, matrix products, coupled(): jnp.einsum('iknm,ikmc->inc', couplings, near_blocks, precision=lax.Precis...  43.1 us
    ppermute x3, waiting for transfers between devices, extended(): lax.ppermute(lax.slice_in_dim(block, block.shape[dim] - width, None, axis...  38 us
    gather x3, local copies, waits for them, and re-layouts, operate_on(): near = blocks_all[local_index]  15.2 us
    ppermute x3, waiting for transfers between devices, extended(): lax.ppermute(lax.slice_in_dim(block, 0, width, axis=dim), axis, backward)  14.9 us
    another operation x3, other arithmetic, per_device(): factor = jnp.linalg.cholesky(gram)  12.4 us
  transfers between devices with their start and end apart: 9, of which 9 were waited for; matrix products, arithmetic and copies ran while one was open for 1% of the time, Pallas kernels for 0%

commit v1 on v0

--- a/solution.py
+++ b/solution.py
@@ -89,7 +89,8 @@
         )
     contrib = real_part / count * iterate[..., :ncol] - imag_part / count * iterate[..., ncol:]
     contrib = contrib.reshape(rows_here, ncol)
-    field = lax.psum(contrib, "shift")
+    y1 = lax.all_gather(contrib, "shift")
+    field = jnp.sum(y1, axis=0)
     gram = lax.psum(product(field.T, field), "rows") / total
     factor = jnp.linalg.cholesky(gram)
     basis = jax.scipy.linalg.solve_triangular(factor, field.T, lower=True).T

time: 562 us -> 530 us (0.943)
  waiting for transfers between devices: 402 us -> 370 us
    psum x1 -> x0, waiting for transfers between devices: 65 us -> none  [per_device(): field = lax.psum(contrib, 'shift')]
    all_gather x0 -> x1, waiting for transfers between devices: none -> 34.7 us  [per_device(): y1 = lax.all_gather(contrib, 'shift')]
  transfers between devices with their start and end apart: 9 -> 9, of which waited for: 9 -> 9; matrix products, arithmetic and copies ran while one was open for 1% -> 2% of each run, Pallas kernels for 0% -> 0%
where the time goes in v1:
time: 530 us; the launch traced here: 525 us
  waiting for transfers between devices  370 us (70%)
  matrix products  59.4 us (11%)
  other arithmetic  40.1 us (8%)
  local copies, waits for them, and re-layouts  23.8 us (4%)
  starting transfers between devices  16.5 us (3%)
  between operations  14.5 us (3%)
    psum x1, waiting for transfers between devices, per_device(): gram = lax.psum(product(field.T, field), 'rows') / total  142 us
    psum x1, waiting for transfers between devices, per_device(): projected = lax.psum(product(basis.T, image), 'rows') / total  141 us
    dot_general x3, matrix products, coupled(): jnp.einsum('iknm,ikmc->inc', couplings, near_blocks, precision=lax.Precis...  43.1 us
    ppermute x3, waiting for transfers between devices, extended(): lax.ppermute(lax.slice_in_dim(block, block.shape[dim] - width, None, axis...  38 us
    all_gather x1, waiting for transfers between devices, per_device(): y1 = lax.all_gather(contrib, 'shift')  34.7 us
    gather x3, local copies, waits for them, and re-layouts, operate_on(): near = blocks_all[local_index]  15.2 us
    ppermute x3, waiting for transfers between devices, extended(): lax.ppermute(lax.slice_in_dim(block, 0, width, axis=dim), axis, backward)  14.9 us
    another operation x3, other arithmetic, per_device(): factor = jnp.linalg.cholesky(gram)  12.4 us
  transfers between devices with their start and end apart: 9, of which 9 were waited for; matrix products, arithmetic and copies ran while one was open for 2% of the time, Pallas kernels for 0%

profile of v1, /device:TPU:2, one launch (start us, length us, event | category | flops | bytes accessed | tf_op | source)
XLA Modules:
  0.0 524.5 jit_solution(15951234211599789368)
XLA Ops:
  12.9 4.8 collective-permute-start
  22.3 17.1 %collective-permute-done = f32[1024,256]{1,0:T(8,128)} collective-permute-done((f32[1024,256]{1,0:T(8,128)}, f32[1024,256]{1,0:T(8,128)}, u32[]{:S(2)}, u32[]{:S(2)}) %collective-permute-start) | collective-permute-done | bytes 1048608 | tf_op jit(solution)/shard_map/ppermute | solution.py:16
  39.4 5.1 collective-permute-done.1
  44.5 3.8 pad_maximum_fusion
  48.3 6.2 %gather_fusion = f32[64,128,256]{2,1,0:T(8,128)} fusion(f32[24,128,256]{2,1,0:T(8,128)} %bitcast.107, s32[1024]{0:T(1024)S(1)} %pad_clamp_fusion), kind=kCustom, calls=%fused_computation | custom fusion | bytes 16777472 | tf_op jit(solution)/shard_map/gather | solution.py:72
  54.5 17.7 %fusion.11 = f32[8,128,256]{1,2,0:T(8,128)S(1)} fusion(f32[8,256,128]{2,1,0:T(8,128)S(1)} %fusion.37, f32[8,8,128,256]{3,2,1,0:T(8,128)} %bitcast.110, f32[8,8,128,128]{3,2,1,0:T(8,128)} %param.6, f32[8,128,128]{1,2,0:T(8,128)S(1)} %copy.36, f32[8,128,128]{1,2,0:T(8,128)} %get-tuple-element.21, f32[8,128,128]{1,2,0:T(8,128)} %get-tuple-element.20), kind=kOutput, calls=%fused_computation.26 | convolution fusion | flops 3222274048 | bytes 16252928 | tf_op jit(solution)/shard_map/iknm,ikmc->inc/dot_general | solution.py:52
  75.8 4.0 collective-permute-start.2
  84.3 16.2 %collective-permute-done.2 = f32[1024,256]{1,0:T(8,128)} collective-permute-done((f32[1024,256]{1,0:T(8,128)}, f32[1024,256]{1,0:T(8,128)}, u32[]{:S(2)}, u32[]{:S(2)}) %collective-permute-start.2) | collective-permute-done | bytes 1048608 | tf_op jit(solution)/shard_map/ppermute | solution.py:16
  100.6 5.6 %collective-permute-done.3 = f32[1024,256]{1,0:T(8,128)} collective-permute-done((f32[1024,256]{1,0:T(8,128)}, f32[1024,256]{1,0:T(8,128)}, u32[]{:S(2)}, u32[]{:S(2)}) %collective-permute-start.3) | collective-permute-done | bytes 1048608 | tf_op jit(solution)/shard_map/ppermute | solution.py:19
  106.2 3.8 pad_maximum_fusion.1
  110.0 6.2 %gather_fusion.1 = f32[64,128,256]{2,1,0:T(8,128)} fusion(f32[24,128,256]{2,1,0:T(8,128)} %bitcast.108, s32[1024]{0:T(1024)S(1)} %pad_clamp_fusion), kind=kCustom, calls=%fused_computation.1 | custom fusion | bytes 16777472 | tf_op jit(solution)/shard_map/gather | solution.py:72
  116.2 17.3 %fusion.14 = f32[8,128,256]{1,2,0:T(8,128)S(1)} fusion(f32[8,256,128]{2,1,0:T(8,128)S(1)} %fusion.38, f32[8,8,128,256]{3,2,1,0:T(8,128)} %bitcast.109, f32[8,8,128,128]{3,2,1,0:T(8,128)} %param.6, f32[8,128,128]{1,2,0:T(8,128)S(1)} %copy.36, f32[8,128,128]{1,2,0:T(8,128)} %get-tuple-element.19, f32[8,128,128]{1,2,0:T(8,128)} %get-tuple-element.18), kind=kOutput, calls=%fused_computation.29 | convolution fusion | flops 3222274048 | bytes 16252928 | tf_op jit(solution)/shard_map/iknm,ikmc->inc/dot_general | solution.py:52
  137.0 34.7 %all-gather.2.cloned.1.call-done = f32[8,1024,128]{2,1,0:T(8,128)} async-done(((f32[1,1024,128]{2,1,0:T(8,128)}), f32[8,1024,128]{2,1,0:T(8,128)}) %all-gather.2.cloned.1.call-update) | async-done | bytes 4194320 | tf_op jit(solution)/shard_map/all_gather | solution.py:92
  171.7 2.4 reduce_sum.9
  176.0 142.1 %all-reduce.4.cloned.1.call-done = f32[128,128]{0,1:T(8,128)} async-done(((f32[128,128]{0,1:T(8,128)}), f32[128,128]{0,1:T(8,128)}) %all-reduce.4.cloned.1.call-update) | async-done | bytes 65552 | tf_op jit(solution)/shard_map/psum | solution.py:94
  320.0 11.7 %cholesky.16 = f32[128,128]{1,0:T(8,128)S(1)} custom-call(f32[128,128]{1,0:T(8,128)S(1)} %fusion.30), custom_call_target="Cholesky" | custom-call | tf_op jit(solution)/shard_map/jit(cholesky)/cholesky | solution.py:95
  333.0 9.8 %custom-call.7 = f32[1,128,128]{1,2,0:T(8,128)S(1)} custom-call(f32[1,128,128]{2,1,0:T(8,128)S(1)} %fusion.27), custom_call_target="InvertDiagBlocksLowerTriangular" | custom-call | tf_op jit(solution)/shard_map/jit(_solve_triangular)/triangular_solve | solution.py:96
  343.5 3.2 collective-permute-start.4
  348.9 4.7 collective-permute-done.4
  353.6 4.2 collective-permute-done.5
  359.0 1.9 copy.66
  360.9 2.8 gather_fusion.2
  363.7 8.1 %convolution_bitcast_fusion.4 = f32[8,128,128]{1,2,0:T(8,128)S(1)} fusion(f32[8,8,128,128]{3,2,1,0:T(8,128)} %bitcast.114, f32[8,8,128,128]{3,2,1,0:T(8,128)} %param.6), kind=kOutput, calls=%fused_computation.30 | convolution fusion | flops 1610612736 | bytes 8912896 | tf_op jit(solution)/shard_map/iknm,ikmc->inc/dot_general | solution.py:52
  375.6 140.5 %all-reduce.6.cloned.1.call-done = f32[128,128]{0,1:T(8,128)} async-done(((f32[128,128]{0,1:T(8,128)}), f32[128,128]{0,1:T(8,128)}) %all-reduce.6.cloned.1.call-update) | async-done | bytes 65552 | tf_op jit(solution)/shard_map/psum | solution.py:99
  (56 shorter events, 36.2 us)
Async XLA Ops:
  7.2 1.5 copy-start
  7.2 164.5 %all-gather.2.cloned.1.call-start = ((), (), s32[]{:S(2)}) async-start(), calls=%async_computation | async-start | bytes 4718592 | tf_op jit(solution)/shard_map/all_gather | solution.py:92
  8.6 10.3 %copy-start.3 = (s32[8,8]{1,0:T(8,128)S(1)}, s32[8,8]{1,0:T(8,128)}, u32[]{:S(2)}) copy-start(s32[8,8]{1,0:T(8,128)} %param.5) | copy-start | bytes 772
  10.3 9.9 %copy-start.2 = (f32[8,128]{1,0:T(8,128)S(1)}, f32[8,128]{1,0:T(8,128)}, u32[]{:S(2)}) copy-start(f32[8,128]{1,0:T(8,128)} %param.8) | copy-start | bytes 12292
  12.9 26.5 %collective-permute-start = (f32[1024,256]{1,0:T(8,128)}, f32[1024,256]{1,0:T(8,128)}, u32[]{:S(2)}, u32[]{:S(2)}) collective-permute-start(f32[1024,256]{1,0:T(8,128)} %bitcast.3), channel_id=1, source_target_pairs={{0,1},{1,2},{2,3},{3,4},{4,5},{5,6},{6,7},{7,8},{8,9},{9,10},{10,1... | collective-permute-start | bytes 3145736 | tf_op jit(solution)/shard_map/ppermute | solution.py:16
  17.7 26.8 %collective-permute-start.1 = (f32[1024,256]{1,0:T(8,128)}, f32[1024,256]{1,0:T(8,128)}, u32[]{:S(2)}, u32[]{:S(2)}) collective-permute-start(f32[1024,256]{1,0:T(8,128)} %bitcast.3), channel_id=1, source_target_pairs={{1,0},{2,1},{3,2},{4,3},{5,4},{6,5},{7,6},{8,7},{9,8},{10,9},{11,1... | collective-permute-start | bytes 3145736 | tf_op jit(solution)/shard_map/ppermute | solution.py:19
  75.8 24.8 %collective-permute-start.2 = (f32[1024,256]{1,0:T(8,128)}, f32[1024,256]{1,0:T(8,128)}, u32[]{:S(2)}, u32[]{:S(2)}) collective-permute-start(f32[1024,256]{1,0:T(8,128)} %bitcast.11), channel_id=1, source_target_pairs={{0,1},{1,2},{2,3},{3,4},{4,5},{5,6},{6,7},{7,8},{8,9},{9,10},{10,1... | collective-permute-start | bytes 3145736 | tf_op jit(solution)/shard_map/ppermute | solution.py:16
  79.8 26.4 %collective-permute-start.3 = (f32[1024,256]{1,0:T(8,128)}, f32[1024,256]{1,0:T(8,128)}, u32[]{:S(2)}, u32[]{:S(2)}) collective-permute-start(f32[1024,256]{1,0:T(8,128)} %bitcast.11), channel_id=1, source_target_pairs={{1,0},{2,1},{3,2},{4,3},{5,4},{6,5},{7,6},{8,7},{9,8},{10,9},{11,1... | collective-permute-start | bytes 3145736 | tf_op jit(solution)/shard_map/ppermute | solution.py:19
  136.9 181.2 %all-reduce.4.cloned.1.call-start = ((), (), s32[]{:S(2)}) async-start(), calls=%async_computation.1 | async-start | bytes 131072 | tf_op jit(solution)/shard_map/psum | solution.py:94
  175.8 340.4 %all-reduce.6.cloned.1.call-start = ((), (), s32[]{:S(2)}) async-start(), calls=%async_computation.2 | async-start | bytes 131072 | tf_op jit(solution)/shard_map/psum | solution.py:99
  343.5 10.1 %collective-permute-start.4 = (f32[1024,128]{0,1:T(8,128)S(1)}, f32[1024,128]{0,1:T(8,128)S(1)}, u32[]{:S(2)}, u32[]{:S(2)}) collective-permute-start(f32[1024,128]{0,1:T(8,128)S(1)} %bitcast.115), channel_id=1, source_target_pairs={{0,1},{1,2},{2,3},{3,4},{4,5},{5,6},{6,7},{7,8},{8,9},{9,10},{10,1... | collective-permute-start | bytes 1572872 | tf_op jit(solution)/shard_map/ppermute | solution.py:16
  346.7 11.1 %collective-permute-start.5 = (f32[1024,128]{0,1:T(8,128)S(1)}, f32[1024,128]{0,1:T(8,128)S(1)}, u32[]{:S(2)}, u32[]{:S(2)}) collective-permute-start(f32[1024,128]{0,1:T(8,128)S(1)} %bitcast.116), channel_id=1, source_target_pairs={{1,0},{2,1},{3,2},{4,3},{5,4},{6,5},{7,6},{8,7},{9,8},{10,9},{11,1... | collective-permute-start | bytes 1572872 | tf_op jit(solution)/shard_map/ppermute | solution.py:19
  373.0 144.7 %copy-start.1 = (f32[8,128,128]{1,2,0:T(8,128)}, f32[8,128,128]{1,2,0:T(8,128)S(1)}, u32[]{:S(2)}) copy-start(f32[8,128,128]{1,2,0:T(8,128)S(1)} %convolution_add_fusion) | copy-start | bytes 1572868
Sparse Core Ops, SparseCore 0:
  137.1 34.5 all-gather.1
  175.9 142.2 all-reduce.3
  374.7 141.3 all-reduce.5
